TPU v7x, 32 devices: a whole 2x2x4 slice. The times are simulated.
32 devices in a mesh: group: 16 (over z, y, core), tp: 2 (over x).
Axes of the slice: x: 2, y: 2, z: 4, core: 2. Of those that a mesh axis runs over, the one named last changes fastest.
Arguments:
- tokens: bfloat16 [8192, 3200], P('group', 'tp'), may hold values from -6 to 6
- norm_gain: bfloat16 [3200], P('tp'), may hold values from 0.25 to 1.75
- w_qkv: bfloat16 [3200, 3, 2048], P('group', None, 'tp'), may hold values from -1 to 1, as said below
- qk_gain: float32 [2, 2048], P(None, 'tp'), may hold values from 0.5 to 8
- w_out: bfloat16 [2048, 3200], P('tp', 'group'), may hold values from -0.125 to 0.125
- layer_scale: float32 [3200], P('tp'), may hold values from 0.3 to 1.5
- request: int32 [8192], P('group'), may hold values from 0 to 8191, as said below
- owner: int32 [8192, 1], P('group'), may hold values from 0 to 15; in each aligned block of 512 rows (0 to 511, 512 to 1023, ...) at most 64 rows name the same one
Outputs:
- routed: bfloat16 [16, 16, 64, 3200], P('group', None, None, 'tp')
Inputs may be any that keep to these rules, and one draw needn't show every extreme that they name: Requests never cross a block of 1024 rows starting at a multiple of 1024, and blocks share none; in each such block exactly one request holds rows on both sides of its middle, at most 128 on each side, exactly 128 on each side in the first block; the first row's number is 0 and the last row's is 8191. Among one group's 512 rows at most 64 name the same owner; some owner is named by exactly 64 rows of some group. `w_qkv`: column scales of the projections vary across the columns.
All inputs are finite; a program needn't handle non-finite values.
Results may differ from a plain program's by a relative error of at most 0.0117.
The roundings to bfloat16 on the way count: a program that leaves them out, or rounds other values in their place, can miss the bound.
Values may be sent and summed in bfloat16 or wider, within the bound.
A program may use at most 128 MiB of HBM per device.

v0:
```python
import math
import jax
import jax.numpy as jnp
from jax import lax
from jax.sharding import PartitionSpec as P

HD = 128
SHARE = 128


def swapped(value, axis, apart):
    mask = 2**apart
    pairs = [(source, source ^ mask) for source in range(lax.axis_size(axis))]
    return lax.ppermute(value, axis, pairs)


def from_next(value, axis):
    count = lax.axis_size(axis)
    return lax.ppermute(value, axis, [((i + 1) % count, i) for i in range(count)])


def shards(tokens, norm_gain, w_qkv, qk_gain, w_out, layer_scale, request, owner):
    rows, feat_local = tokens.shape
    tp_count = lax.axis_size("tp")
    group_count = lax.axis_size("group")
    local_width = w_qkv.shape[2]
    head_count = local_width // HD
    me_tp = lax.axis_index("tp")
    w_k, w_q = (lax.all_gather(w_qkv[:, i, :], "group", axis=0, tiled=True) for i in (1, 0))
    whole = jnp.zeros((rows, feat_local * tp_count), jnp.bfloat16)
    gain_all = jnp.zeros((1, feat_local * tp_count), jnp.bfloat16)
    piece, gain = (tokens, norm_gain.reshape(1, feat_local))
    for step in range(tp_count):
        at = (me_tp + step) % tp_count * feat_local
        whole = lax.dynamic_update_slice(whole, piece, (0, at))
        gain_all = lax.dynamic_update_slice(gain_all, gain, (0, at))
        if step < tp_count - 1:
            piece, gain = (from_next(piece, "tp"), from_next(gain, "tp"))
    whole, late_v, late_out = lax.optimization_barrier((whole, w_qkv[:, 2, :], w_out))
    w_v = lax.all_gather(late_v, "group", axis=0, tiled=True)
    per = group_count // tp_count
    pairs = []
    for g in range(group_count):
        for b in range(tp_count):
            t, j = (g // per, g % per)
            to_g = (b - t) % tp_count * per + j
            pairs.append((g * tp_count + b, to_g * tp_count + t))
    w_piece = lax.ppermute(late_out.T, ("group", "tp"), pairs)
    w_o = lax.all_gather(w_piece, "group", axis=0, tiled=True)
    w_o = w_o.reshape(tp_count, feat_local, local_width)
    xwide = whole.astype(jnp.float32)
    stat = jnp.mean(xwide * xwide, axis=-1, keepdims=True)
    normed = (xwide * lax.rsqrt(stat + 1e-06) * gain_all.astype(jnp.float32)).astype(jnp.bfloat16)
    key_rows = jnp.dot(normed, w_k, preferred_element_type=jnp.float32)
    query = jnp.dot(normed, w_q, preferred_element_type=jnp.float32)
    qsum, ksum = lax.psum(
        (jnp.sum(query * query, axis=-1), jnp.sum(key_rows * key_rows, axis=-1)), "tp"
    )
    total_width = local_width * tp_count
    qnorm = (query * lax.rsqrt(qsum / total_width + 1e-06)[:, None] * qk_gain[0]).astype(
        jnp.bfloat16
    )
    knorm = (key_rows * lax.rsqrt(ksum / total_width + 1e-06)[:, None] * qk_gain[1]).astype(
        jnp.bfloat16
    )
    parity = lax.axis_index("group") % 2
    seam = jnp.where(parity == 0, rows - SHARE, 0).astype(jnp.int32)
    key_window = lax.dynamic_slice_in_dim(knorm, seam, SHARE, 0)
    id_window = lax.dynamic_slice_in_dim(request, seam, SHARE, 0)
    paired_key, paired_ids = swapped((key_window, id_window), "group", 0)
    all_keys = jnp.concatenate([knorm, paired_key], axis=0)
    all_ids = jnp.concatenate([request, paired_ids], axis=0)
    qheads = qnorm.reshape(rows, head_count, HD)
    kheads = all_keys.reshape(rows + SHARE, head_count, HD)
    scores = jnp.einsum(
        "qhd,khd->hqk", qheads, kheads, preferred_element_type=jnp.float32
    ) / math.sqrt(HD)
    same = request[:, None] == all_ids[None, :]
    scores = jnp.where(same[None], scores, -jnp.inf)
    top = jnp.max(scores, axis=-1, keepdims=True)
    expo = jnp.exp(scores - top)
    probs = (expo / jnp.sum(expo, axis=-1, keepdims=True)).astype(jnp.bfloat16)
    value = jnp.dot(normed, w_v, preferred_element_type=jnp.float32).astype(jnp.bfloat16)
    value_window = lax.dynamic_slice_in_dim(value, seam, SHARE, 0)
    all_values = jnp.concatenate([value, swapped(value_window, "group", 0)], axis=0)
    vheads = all_values.reshape(rows + SHARE, head_count, HD)
    attended = jnp.einsum("hqk,khd->qhd", probs, vheads, preferred_element_type=jnp.float32)
    attended = attended.astype(jnp.bfloat16).reshape(rows, local_width)
    branch = jnp.zeros((rows, feat_local), jnp.float32)
    for step in range(tp_count):
        onward = from_next(attended, "tp") if step < tp_count - 1 else None
        part = lax.dot_general(
            attended, w_o[step], (((1,), (1,)), ((), ())), preferred_element_type=jnp.float32
        )
        branch = branch + part.astype(jnp.bfloat16).astype(jnp.float32)
        attended = onward
    mixed = (tokens.astype(jnp.float32) + layer_scale * branch).astype(jnp.bfloat16)
    capacity = max(2, 2 * rows // group_count)
    target = owner[:, 0]
    onehot = (target[:, None] == jnp.arange(group_count, dtype=jnp.int32)[None, :]).astype(
        jnp.int32
    )
    slot = jnp.sum((jnp.cumsum(onehot, axis=0) - onehot) * onehot, axis=-1)
    place = target * capacity + slot
    select = (
        jnp.arange(group_count * capacity, dtype=jnp.int32)[:, None] == place[None, :]
    ).astype(jnp.bfloat16)
    outbox = jnp.dot(select, mixed, preferred_element_type=jnp.float32).astype(jnp.bfloat16)
    outbox = outbox.reshape(group_count, capacity, feat_local)
    inbox = lax.all_to_all(outbox, "group", split_axis=0, concat_axis=0, tiled=True)
    return inbox[None]


def solution(mesh):
    in_specs = (
        P("group", "tp"),
        P("tp"),
        P("group", None, "tp"),
        P(None, "tp"),
        P("tp", "group"),
        P("tp"),
        P("group"),
        P("group", None),
    )
    out_specs = P("group", None, None, "tp")
    return jax.shard_map(shards, mesh=mesh, in_specs=in_specs, out_specs=out_specs, check_vma=False)
```

profile of v0, /device:TPU:1, one launch (start us, length us, event | category | flops | bytes accessed | tf_op | source)
XLA Modules:
  0.0 388.7 jit_solution(6893190634772849694)
XLA Ops:
  6.5 0.0 all-gather.13.cloned.1.call-start
  6.5 2.3 fusion.44
  8.8 0.0 all-gather.13.cloned.1.call-update
  8.9 0.0 all-gather.11.cloned.1.call-start
  8.9 0.7 all-gather.11.cloned.1.call-update
  9.6 0.0 all-gather.7.cloned.1.call-start
  9.7 2.1 collective-permute-start
  11.8 0.2 broadcast_in_dim.16
  12.0 0.0 copy-start.3
  12.0 0.0 copy-start.4
  12.0 0.0 copy-start.5
  12.0 1.6 constant_dynamic-update-slice_fusion.1
  13.6 34.0 %collective-permute-done = bf16[512,1600]{0,1:T(8,128)(2,1)} collective-permute-done((bf16[512,1600]{0,1:T(8,128)(2,1)}, bf16[512,1600]{0,1:T(8,128)(2,1)}, u32[]{:S(2)}, u32[]{:S(2)}) %collective-permute-start) | collective-permute-done | bytes 1638432 | tf_op jit(solution)/shard_map/ppermute | solution.py:19
  47.6 1.6 constant_dynamic-update-slice_fusion
  49.2 0.0 all-gather.7.cloned.1.call-update
  49.2 0.0 all-gather.9.cloned.1.call-start
  49.3 4.9 %collective-permute-start.5 = (bf16[200,1024]{1,0:T(8,128)(2,1)}, bf16[200,1024]{1,0:T(8,128)(2,1)}, u32[]{:S(2)}, u32[]{:S(2)}) collective-permute-start(bf16[200,1024]{1,0:T(8,128)(2,1)} %bitcast.70), channel_id=1, source_target_pairs={{0,0},{1,16},{2,2},{3,18},{4,4},{5,20},{6,6},{7,22},{8,8},{9,24},{... | collective-permute-start | bytes 1228808 | tf_op jit(solution)/shard_map/ppermute | solution.py:48
  54.2 0.0 collective-permute-done.5
  54.2 0.0 all-gather.9.cloned.1.call-update
  54.2 0.0 copy-done.3
  54.2 35.8 %collective-permute-start.1 = (bf16[1,1600]{1,0:T(2,128)(2,1)S(1)}, bf16[1,1600]{1,0:T(2,128)(2,1)S(1)}, u32[]{:S(2)}, u32[]{:S(2)}) collective-permute-start(bf16[1,1600]{1,0:T(2,128)(2,1)S(1)} %reshape.93), channel_id=1, source_target_pairs={{1,0},{0,1},{3,2},{2,3},{5,4},{4,5},{7,6},{6,7},{9,8},{8,9},{11,10... | collective-permute-start | bytes 9608 | tf_op jit(solution)/shard_map/ppermute | solution.py:19
  90.0 0.0 copy-done.4
  90.0 0.1 dynamic_slice.10
  90.1 0.9 collective-permute-start.3
  91.0 0.0 copy-done.5
  91.1 0.3 dynamic_update_slice.16
  91.4 0.5 collective-permute-done.3
  91.9 0.0 collective-permute-done.1
  91.9 0.3 dynamic_update_slice.17
  92.2 0.8 fusion.2
  93.0 0.0 all-gather.13.cloned.1.call-done
  93.0 8.0 %multiply_reduce_fusion = (f32[512]{0:T(512)S(1)}, f32[512,1024]{1,0:T(8,128)}) fusion(bf16[3200,1,1024]{2,0,1:T(8,128)(2,1)} %all-gather.13.cloned.1.call-done, bf16[512,3200]{0,1:T(8,128)(2,1)S(1)} %constant_dynamic-update-slice_fusion, f32[3200]{0:T(1024)S(1)} %mul.106, f32[512]{0:T(512)S(1)} %add_rsqrt_fusion.2), kind=kOutput, calls=%fused_computation.27 | convolution fusion | flops 3363044864 | bytes 11944448 | tf_op jit(solution)/shard_map/dot_general | solution.py:54
  101.0 53.1 %all-gather.11.cloned.1.call-done = bf16[3200,1,1024]{2,0,1:T(8,128)(2,1)} async-done(((bf16[200,1,1024]{2,0,1:T(8,128)(2,1)}), bf16[3200,1,1024]{2,0,1:T(8,128)(2,1)}) %all-gather.11.cloned.1.call-update) | async-done | bytes 6553616 | tf_op jit(solution)/shard_map/all_gather | solution.py:29
  154.1 8.0 %multiply_reduce_fusion.1 = (f32[512]{0:T(512)S(1)}, f32[512,1024]{1,0:T(8,128)}) fusion(bf16[3200,1,1024]{2,0,1:T(8,128)(2,1)} %all-gather.11.cloned.1.call-done, bf16[512,3200]{0,1:T(8,128)(2,1)S(1)} %constant_dynamic-update-slice_fusion, f32[3200]{0:T(1024)S(1)} %mul.106, f32[512]{0:T(512)S(1)} %add_rsqrt_fusion.2), kind=kOutput, calls=%fused_computation.29 | convolution fusion | flops 3363044864 | bytes 11944448 | tf_op jit(solution)/shard_map/dot_general | solution.py:55
  162.1 4.3 %all-reduce = (f32[512]{0:T(512)S(1)}, f32[512]{0:T(512)S(1)}) all-reduce(f32[512]{0:T(512)S(1)} %get-tuple-element.18, f32[512]{0:T(512)S(1)} %get-tuple-element.20), channel_id=1, replica_groups=mesh['group'=16,'tp'=2] {'tp'}, use_global_device_ids=true, to_apply=%region_7.8 | all-reduce | flops 1024 | bytes 8192 | tf_op jit(solution)/shard_map/psum | solution.py:56
  166.4 2.0 multiply_convert_fusion
  168.5 1.1 collective-permute-start.4
  169.5 1.0 broadcast_compare_fusion
  170.5 0.2 collective-permute-done.4
  170.7 0.0 copy-done
  170.7 5.6 %fusion.26 = f32[8,512,640]{2,1,0:T(8,128)} fusion(bf16[128,1024]{1,0:T(8,128)(2,1)S(1)} %collective-permute-done.4, bf16[512,1024]{1,0:T(8,128)(2,1)S(1)} %multiply_convert_fusion, f32[512,1024]{1,0:T(8,128)S(1)} %copy-done, f32[1024]{0:T(1024)S(1)} %bitcast.66, f32[512]{0:T(512)S(1)} %add_rsqrt_fusion.1), kind=kOutput, calls=%fused_computation.33 | convolution fusion | flops 675282944 | bytes 13899776 | tf_op jit(solution)/shard_map/qhd,khd->hqk/dot_general | solution.py:75
  176.3 42.1 %all-gather.7.cloned.1.call-done = bf16[3200,1024]{1,0:T(8,128)(2,1)} async-done(((bf16[200,1024]{1,0:T(8,128)(2,1)}), bf16[3200,1024]{1,0:T(8,128)(2,1)}) %all-gather.7.cloned.1.call-update) | async-done | bytes 6553616 | tf_op jit(solution)/shard_map/all_gather | solution.py:40
  218.3 6.7 %convolution_convert_fusion.1 = bf16[512,1024]{1,0:T(8,128)(2,1)S(1)} fusion(bf16[3200,1024]{1,0:T(8,128)(2,1)} %all-gather.7.cloned.1.call-done, bf16[512,3200]{0,1:T(8,128)(2,1)S(1)} %constant_dynamic-update-slice_fusion, f32[3200]{0:T(1024)S(1)} %mul.106, f32[512]{0:T(512)S(1)} %add_rsqrt_fusion.2), kind=kOutput, calls=%fused_computation.32 | convolution fusion | flops 3362521088 | bytes 10893824 | tf_op jit(solution)/shard_map/dot_general | solution.py:83
  225.1 0.3 collective-permute-start.2
  225.4 0.0 copy-done.1
  225.4 15.4 %fusion.46 = (f32[8,512]{1,0:T(8,128)S(1)}, f32[8,512,640]{2,1,0:T(8,128)}) fusion(f32[8,512,640]{2,1,0:T(8,128)} %fusion.26, pred[512,640]{1,0:T(8,128)(4,1)S(1)} %copy-done.1), kind=kOutput, calls=%fused_computation.66 | output fusion | flops 15729279 | bytes 21315584 | tf_op jit(solution)/shard_map/sub | solution.py:81
  240.8 0.0 collective-permute-done.2
  240.8 0.1 pad_maximum_fusion
  240.9 1.0 copy.18
  241.9 0.0 copy-start.2
  241.9 6.0 %fusion.25 = bf16[8,128,512]{2,1,0:T(8,128)(2,1)S(1)} fusion(bf16[640,8,128]{0,2,1:T(8,128)(2,1)S(1)} %bitcast.62, f32[8,512,640]{2,1,0:T(8,128)} %get-tuple-element.23, f32[8,512]{1,0:T(8,128)S(1)} %get-tuple-element.22), kind=kOutput, calls=%fused_computation.31 | convolution fusion | flops 676855808 | bytes 12861440 | tf_op jit(solution)/shard_map/hqk,khd->qhd/dot_general | solution.py:87
  247.9 1.3 collective-permute-start.6
  249.2 0.0 copy-done.2
  249.2 1.2 reduce-window.6
  250.3 0.2 slice_reduce_fusion
  250.6 0.1 fusion.37
  250.7 0.0 copy-start.6
  250.7 31.7 %all-gather.9.cloned.1.call-done = bf16[3200,1024]{1,0:T(8,128)(2,1)} async-done(((bf16[200,1024]{1,0:T(8,128)(2,1)}), bf16[3200,1024]{1,0:T(8,128)(2,1)}) %all-gather.9.cloned.1.call-update) | async-done | bytes 6553616 | tf_op jit(solution)/shard_map/all_gather | solution.py:49
  282.4 5.0 %fusion.17 = bf16[512,1600]{0,1:T(8,128)(2,1)} fusion(bf16[512,1024]{0,1:T(8,128)(2,1)S(1)} %bitcast.69, bf16[3200,1024]{1,0:T(8,128)(2,1)} %all-gather.9.cloned.1.call-done), kind=kOutput, calls=%fused_computation.24 | convolution fusion | flops 1678540800 | bytes 5963776 | tf_op jit(solution)/shard_map/dot_general | solution.py:92
  287.4 0.0 collective-permute-done.6
  287.4 8.5 %convolution_convert_fusion = bf16[1024,1600]{0,1:T(8,128)(2,1)} fusion(s32[512]{0:T(512)S(1)} %multiply_add_fusion, bf16[512,1600]{0,1:T(8,128)(2,1)} %fusion.17, bf16[512,1600]{0,1:T(8,128)(2,1)} %param.8, bf16[512,1024]{0,1:T(8,128)(2,1)S(1)} %collective-permute-done.6, bf16[3200,1024]{1,0:T(8,128)(2,1)} %all-gather.9.cloned.1.call-done, ...), kind=kOutput, calls=%fused_computation.18 | convolution fusion | flops 3364159488 | bytes 10887424 | tf_op jit(solution)/shard_map/dot_general | solution.py:108
  295.9 4.3 %copy.17 = bf16[1024,1600]{1,0:T(8,128)(2,1)S(1)} copy(bf16[1024,1600]{0,1:T(8,128)(2,1)} %convolution_convert_fusion) | data formatting | bytes 6553600 | tf_op jit(solution)/shard_map/convert_element_type | solution.py:108
  300.3 80.1 %all_to_all.5 = bf16[16,64,1600]{2,1,0:T(8,128)(2,1)S(1)} all-to-all(bf16[16,64,1600]{2,1,0:T(8,128)(2,1)S(1)} %bitcast.60), channel_id=1, replica_groups=mesh['group'=16,'tp'=2] {'group'}, dimensions={0} | all-to-all | bytes 6553600 | tf_op jit(solution)/shard_map/all_to_all | solution.py:110
  380.4 1.8 copy.36
  (18 shorter events, 0.2 us)
Async XLA Ops:
  6.5 86.5 %all-gather.13.cloned.1.call-start = ((), (), s32[]{:S(2)}) async-start(), calls=%async_computation.4 | async-start | bytes 6963200 | tf_op jit(solution)/shard_map/all_gather | solution.py:29
  8.9 145.2 %all-gather.11.cloned.1.call-start = ((), (), s32[]{:S(2)}) async-start(), calls=%async_computation.3 | async-start | bytes 6963200 | tf_op jit(solution)/shard_map/all_gather | solution.py:29
  9.6 208.7 %all-gather.7.cloned.1.call-start = ((), (), s32[]{:S(2)}) async-start(), calls=%async_computation.1 | async-start | bytes 6963200 | tf_op jit(solution)/shard_map/all_gather | solution.py:40
  9.7 38.0 %collective-permute-start = (bf16[512,1600]{0,1:T(8,128)(2,1)}, bf16[512,1600]{0,1:T(8,128)(2,1)}, u32[]{:S(2)}, u32[]{:S(2)}) collective-permute-start(bf16[512,1600]{0,1:T(8,128)(2,1)} %param.8), channel_id=1, source_target_pairs={{1,0},{0,1},{3,2},{2,3},{5,4},{4,5},{7,6},{6,7},{9,8},{8,9},{11,10... | collective-permute-start | bytes 4915208 | tf_op jit(solution)/shard_map/ppermute | solution.py:19
  12.0 42.2 %copy-start.3 = (bf16[1600]{0:T(1024)(128)(2,1)S(1)}, bf16[1600]{0:T(1024)(128)(2,1)}, u32[]{:S(2)}) copy-start(bf16[1600]{0:T(1024)(128)(2,1)} %param.9) | copy-start | bytes 9604
  12.0 78.0 %copy-start.4 = (s32[512]{0:T(512)S(1)}, s32[512]{0:T(512)}, u32[]{:S(2)}) copy-start(s32[512]{0:T(512)} %param.14) | copy-start | bytes 6148
  12.0 79.0 %copy-start.5 = (f32[2,1024]{1,0:T(2,128)S(1)}, f32[2,1024]{1,0:T(2,128)}, u32[]{:S(2)}) copy-start(f32[2,1024]{1,0:T(2,128)} %param.11) | copy-start | bytes 24580
  49.2 233.2 %all-gather.9.cloned.1.call-start = ((), (), s32[]{:S(2)}) async-start(), calls=%async_computation.2 | async-start | bytes 6963200 | tf_op jit(solution)/shard_map/all_gather | solution.py:49
  49.3 4.9 %collective-permute-start.5 = (bf16[200,1024]{1,0:T(8,128)(2,1)}, bf16[200,1024]{1,0:T(8,128)(2,1)}, u32[]{:S(2)}, u32[]{:S(2)}) collective-permute-start(bf16[200,1024]{1,0:T(8,128)(2,1)} %bitcast.70), channel_id=1, source_target_pairs={{0,0},{1,16},{2,2},{3,18},{4,4},{5,20},{6,6},{7,22},{8,8},{9,24},{... | collective-permute-start | bytes 1228808 | tf_op jit(solution)/shard_map/ppermute | solution.py:48
  54.2 37.6 %collective-permute-start.1 = (bf16[1,1600]{1,0:T(2,128)(2,1)S(1)}, bf16[1,1600]{1,0:T(2,128)(2,1)S(1)}, u32[]{:S(2)}, u32[]{:S(2)}) collective-permute-start(bf16[1,1600]{1,0:T(2,128)(2,1)S(1)} %reshape.93), channel_id=1, source_target_pairs={{1,0},{0,1},{3,2},{2,3},{5,4},{4,5},{7,6},{6,7},{9,8},{8,9},{11,10... | collective-permute-start | bytes 9608 | tf_op jit(solution)/shard_map/ppermute | solution.py:19
  90.1 1.8 collective-permute-start.3
  166.4 4.3 %copy-start = (f32[512,1024]{1,0:T(8,128)S(1)}, f32[512,1024]{1,0:T(8,128)}, u32[]{:S(2)}) copy-start(f32[512,1024]{1,0:T(8,128)} %get-tuple-element.21) | copy-start | bytes 6291460
  168.5 2.2 collective-permute-start.4
  218.3 7.1 %copy-start.1 = (pred[512,640]{1,0:T(8,128)(4,1)S(1)}, pred[512,640]{1,0:T(8,128)(4,1)}, u32[]{:S(2)}) copy-start(pred[512,640]{1,0:T(8,128)(4,1)} %broadcast_compare_fusion) | copy-start | bytes 983044
  225.1 15.7 %collective-permute-start.2 = (bf16[128,1024]{1,0:T(8,128)(2,1)S(1)}, bf16[128,1024]{1,0:T(8,128)(2,1)S(1)}, u32[]{:S(2)}, u32[]{:S(2)}) collective-permute-start(bf16[128,1024]{1,0:T(8,128)(2,1)S(1)} %constant_dynamic-slice_fusion.1), channel_id=1, source_target_pairs={{0,2},{2,0},{4,6},{6,4},{8,10},{10,8},{12,14},{14,12},{16,18},{18,... | collective-permute-start | bytes 786440 | tf_op jit(solution)/shard_map/ppermute | solution.py:14
  241.9 7.3 %copy-start.2 = (s32[512,1]{0,1:T(1,128)S(1)}, s32[512,1]{0,1:T(1,128)}, u32[]{:S(2)}) copy-start(s32[512,1]{0,1:T(1,128)} %param.15) | copy-start | bytes 6148
  247.9 39.5 %collective-permute-start.6 = (bf16[512,1024]{0,1:T(8,128)(2,1)S(1)}, bf16[512,1024]{0,1:T(8,128)(2,1)S(1)}, u32[]{:S(2)}, u32[]{:S(2)}) collective-permute-start(bf16[512,1024]{0,1:T(8,128)(2,1)S(1)} %bitcast.68), channel_id=1, source_target_pairs={{1,0},{0,1},{3,2},{2,3},{5,4},{4,5},{7,6},{6,7},{9,8},{8,9},{11,10... | collective-permute-start | bytes 3145736 | tf_op jit(solution)/shard_map/ppermute | solution.py:19
  250.7 36.7 %copy-start.6 = (f32[1600]{0:T(1024)S(1)}, f32[1600]{0:T(1024)}, u32[]{:S(2)}) copy-start(f32[1600]{0:T(1024)} %param.13) | copy-start | bytes 19204
Sparse Core Ops, SparseCore 0:
  9.6 65.8 all-gather.12
  77.9 76.1 all-gather.10
  156.3 61.9 all-gather.6
  220.5 61.8 all-gather.8
where the time goes:
time: 389 us
  waiting for transfers between devices  162 us (42%)
  blocking collectives  84.5 us (22%)
  matrix products  47.7 us (12%)
  starting transfers between devices  46.6 us (12%)
  other arithmetic  20.6 us (5%)
  local copies, waits for them, and re-layouts  13.7 us (4%)
  between operations  13.3 us (3%)
    all_to_all x1, blocking collectives, shards(): lax.all_to_all(outbox, 'group', split_axis=0, concat_axis=0, tiled=True)  80.1 us
    all_gather x2, waiting for transfers between devices, shards(): lax.all_gather(w_qkv[:, i, :], 'group', axis=0, tiled=True)  53.1 us
    all_gather x1, waiting for transfers between devices, shards(): w_v = lax.all_gather(late_v, 'group', axis=0, tiled=True)  42.1 us
    ppermute x3, starting transfers between devices, from_next(): lax.ppermute(value, axis, [((i + 1) % count, i) for i in range(count)])  39.2 us
    ppermute x3, waiting for transfers between devices, from_next(): lax.ppermute(value, axis, [((i + 1) % count, i) for i in range(count)])  34 us
    all_gather x1, waiting for transfers between devices, shards(): w_o = lax.all_gather(w_piece, 'group', axis=0, tiled=True)  31.7 us
    sub x1, other arithmetic, shards(): expo = jnp.exp(scores - top)  15.4 us
    dot_general x1, matrix products, shards(): jnp.dot(select, mixed, preferred_element_type=jnp.float32)  8.52 us
  transfers between devices with their start and end apart: 11, of which 6 were waited for; matrix products, arithmetic and copies ran while one was open for 17% of the time, Pallas kernels for 0%

commit v1 on v0

--- a/solution.py
+++ b/solution.py
@@ -37,7 +37,6 @@
         if step < tp_count - 1:
             piece, gain = (from_next(piece, "tp"), from_next(gain, "tp"))
     whole, late_v, late_out = lax.optimization_barrier((whole, w_qkv[:, 2, :], w_out))
-    w_v = lax.all_gather(late_v, "group", axis=0, tiled=True)
     per = group_count // tp_count
     pairs = []
     for g in range(group_count):
@@ -46,7 +45,12 @@
             to_g = (b - t) % tp_count * per + j
             pairs.append((g * tp_count + b, to_g * tp_count + t))
     w_piece = lax.ppermute(late_out.T, ("group", "tp"), pairs)
-    w_o = lax.all_gather(w_piece, "group", axis=0, tiled=True)
+
+    def drive_run(point, vec):
+        u_next = jnp.concatenate([point, vec], 1)
+        return jnp.split(lax.all_gather(u_next, "group", axis=0, tiled=True), [point.shape[1]], 1)
+
+    w_v, w_o = drive_run(late_v, w_piece)
     w_o = w_o.reshape(tp_count, feat_local, local_width)
     xwide = whole.astype(jnp.float32)
     stat = jnp.mean(xwide * xwide, axis=-1, keepdims=True)

time: 389 us -> 415 us (1.067)
  waiting for transfers between devices: 162 us -> 187 us
    ppermute x3, waiting for transfers between devices: 34 us -> 50.7 us  [from_next(): lax.ppermute(value, axis, [((i + 1) % count, i) for i in range(count)])]
    all_gather x2 -> x1, waiting for transfers between devices: 73.8 us -> 82.8 us  [drive_run(): lax.all_gather(u_next, 'group', axis=0, tiled=True)]
    ppermute x1, starting transfers between devices: 4.91 us -> 0.69 us  [shards(): w_piece = lax.ppermute(late_out.T, ('group', 'tp'), pairs)]
    ppermute x3, starting transfers between devices: 39.2 us -> 43.4 us  [from_next(): lax.ppermute(value, axis, [((i + 1) % count, i) for i in range(count)])]
  transfers between devices with their start and end apart: 11 -> 10, of which waited for: 6 -> 6; matrix products, arithmetic and copies ran while one was open for 17% -> 13% of each run, Pallas kernels for 0% -> 0%
where the time goes in v1:
time: 415 us; the launch traced here: 414 us
  waiting for transfers between devices  187 us (45%)
  blocking collectives  84.8 us (20%)
  matrix products  47.6 us (11%)
  starting transfers between devices  46.4 us (11%)
  other arithmetic  21.2 us (5%)
  local copies, waits for them, and re-layouts  13.8 us (3%)
  between operations  13.3 us (3%)
    all_gather x1, waiting for transfers between devices, drive_run(): lax.all_gather(u_next, 'group', axis=0, tiled=True)  82.8 us
    all_to_all x1, blocking collectives, shards(): lax.all_to_all(outbox, 'group', split_axis=0, concat_axis=0, tiled=True)  80.4 us
    all_gather x2, waiting for transfers between devices, shards(): lax.all_gather(w_qkv[:, i, :], 'group', axis=0, tiled=True)  52.3 us
    ppermute x3, waiting for transfers between devices, from_next(): lax.ppermute(value, axis, [((i + 1) % count, i) for i in range(count)])  50.7 us
    ppermute x3, starting transfers between devices, from_next(): lax.ppermute(value, axis, [((i + 1) % count, i) for i in range(count)])  43.4 us
    sub x1, other arithmetic, shards(): expo = jnp.exp(scores - top)  15 us
    dot_general x1, matrix products, shards(): jnp.dot(select, mixed, preferred_element_type=jnp.float32)  8.52 us
  transfers between devices with their start and end apart: 10, of which 6 were waited for; matrix products, arithmetic and copies ran while one was open for 13% of the time, Pallas kernels for 0%

profile of v1, /device:TPU:1, one launch (start us, length us, event | category | flops | bytes accessed | tf_op | source)
XLA Modules:
  0.0 414.4 jit_solution(11370718658978917050)
XLA Ops:
  6.5 0.0 all-gather.8.cloned.1.call-start
  6.5 2.3 fusion.49
  8.8 0.0 all-gather.8.cloned.1.call-update
  8.9 0.0 all-gather.10.cloned.1.call-start
  8.9 0.7 all-gather.10.cloned.1.call-update
  9.6 0.0 all-gather.6.cloned.1.call-start
  9.7 2.1 collective-permute-start
  11.8 0.2 broadcast_in_dim.16
  12.0 0.0 copy-start.7
  12.0 0.0 copy-start.1
  12.0 1.7 constant_dynamic-update-slice_fusion.1
  13.7 0.0 copy-start.4
  13.7 0.0 copy-start.5
  13.7 0.0 copy-start.6
  13.7 33.9 %collective-permute-done = bf16[512,1600]{0,1:T(8,128)(2,1)} collective-permute-done((bf16[512,1600]{0,1:T(8,128)(2,1)}, bf16[512,1600]{0,1:T(8,128)(2,1)}, u32[]{:S(2)}, u32[]{:S(2)}) %collective-permute-start) | collective-permute-done | bytes 1638432 | tf_op jit(solution)/shard_map/ppermute | solution.py:19
  47.6 1.6 constant_dynamic-update-slice_fusion
  49.2 0.0 copy-done.7
  49.2 0.7 collective-permute-start.2
  49.9 0.0 collective-permute-done.2
  49.9 0.0 copy-done.1
  49.9 1.0 pad_maximum_fusion.1
  50.9 0.0 all-gather.6.cloned.1.call-update
  50.9 0.0 copy-done.4
  50.9 40.0 %collective-permute-start.1 = (bf16[1,1600]{1,0:T(2,128)(2,1)S(1)}, bf16[1,1600]{1,0:T(2,128)(2,1)S(1)}, u32[]{:S(2)}, u32[]{:S(2)}) collective-permute-start(bf16[1,1600]{1,0:T(2,128)(2,1)S(1)} %reshape.93), channel_id=1, source_target_pairs={{1,0},{0,1},{3,2},{2,3},{5,4},{4,5},{7,6},{6,7},{9,8},{8,9},{11,10... | collective-permute-start | bytes 9608 | tf_op jit(solution)/shard_map/ppermute | solution.py:19
  90.9 0.0 copy-done.5
  90.9 0.1 dynamic_slice.10
  91.0 0.9 collective-permute-start.4
  91.9 0.3 dynamic_update_slice.16
  92.2 0.5 collective-permute-done.4
  92.7 0.0 collective-permute-done.1
  92.8 0.3 dynamic_update_slice.17
  93.1 0.8 fusion.2
  93.8 0.0 all-gather.8.cloned.1.call-done
  93.8 8.0 %multiply_reduce_fusion.1 = (f32[512]{0:T(512)S(1)}, f32[512,1024]{1,0:T(8,128)}) fusion(bf16[3200,1,1024]{2,0,1:T(8,128)(2,1)} %all-gather.8.cloned.1.call-done, bf16[512,3200]{0,1:T(8,128)(2,1)S(1)} %constant_dynamic-update-slice_fusion, f32[3200]{0:T(1024)S(1)} %mul.106, f32[512]{0:T(512)S(1)} %add_rsqrt_fusion.2), kind=kOutput, calls=%fused_computation.31 | convolution fusion | flops 3363044864 | bytes 11944448 | tf_op jit(solution)/shard_map/dot_general | solution.py:59
  101.8 52.3 %all-gather.10.cloned.1.call-done = bf16[3200,1,1024]{2,0,1:T(8,128)(2,1)} async-done(((bf16[200,1,1024]{2,0,1:T(8,128)(2,1)}), bf16[3200,1,1024]{2,0,1:T(8,128)(2,1)}) %all-gather.10.cloned.1.call-update) | async-done | bytes 6553616 | tf_op jit(solution)/shard_map/all_gather | solution.py:29
  154.1 8.0 %multiply_reduce_fusion = (f32[512]{0:T(512)S(1)}, f32[512,1024]{1,0:T(8,128)}) fusion(bf16[3200,1,1024]{2,0,1:T(8,128)(2,1)} %all-gather.10.cloned.1.call-done, bf16[512,3200]{0,1:T(8,128)(2,1)S(1)} %constant_dynamic-update-slice_fusion, f32[3200]{0:T(1024)S(1)} %mul.106, f32[512]{0:T(512)S(1)} %add_rsqrt_fusion.2), kind=kOutput, calls=%fused_computation.29 | convolution fusion | flops 3363044864 | bytes 11944448 | tf_op jit(solution)/shard_map/dot_general | solution.py:58
  162.1 4.3 %all-reduce = (f32[512]{0:T(512)S(1)}, f32[512]{0:T(512)S(1)}) all-reduce(f32[512]{0:T(512)S(1)} %get-tuple-element.18, f32[512]{0:T(512)S(1)} %get-tuple-element.20), channel_id=1, replica_groups=mesh['group'=16,'tp'=2] {'tp'}, use_global_device_ids=true, to_apply=%region_7.8 | all-reduce | flops 1024 | bytes 8192 | tf_op jit(solution)/shard_map/psum | solution.py:60
  166.5 2.0 multiply_convert_fusion
  168.5 1.1 collective-permute-start.5
  169.6 1.0 broadcast_compare_fusion
  170.5 0.2 collective-permute-done.5
  170.7 5.5 %fusion.31 = f32[8,512,640]{2,1,0:T(8,128)} fusion(bf16[128,1024]{1,0:T(8,128)(2,1)S(1)} %collective-permute-done.5, bf16[512,1024]{1,0:T(8,128)(2,1)S(1)} %multiply_convert_fusion, f32[512,1024]{1,0:T(8,128)S(1)} %copy-done, f32[1024]{0:T(1024)S(1)} %bitcast.65, f32[512]{0:T(512)S(1)} %add_rsqrt_fusion.1), kind=kOutput, calls=%fused_computation.35 | convolution fusion | flops 675282944 | bytes 13899776 | tf_op jit(solution)/shard_map/qhd,khd->hqk/dot_general | solution.py:79
  176.2 82.8 %all-gather.6.cloned.1.call-done = bf16[3200,2048]{1,0:T(8,128)(2,1)} async-done(((bf16[200,2048]{1,0:T(8,128)(2,1)}), bf16[3200,2048]{1,0:T(8,128)(2,1)}) %all-gather.6.cloned.1.call-update) | async-done | bytes 13107216 | tf_op jit(solution)/shard_map/all_gather | solution.py:51
  259.0 6.7 %fusion.28 = bf16[512,1024]{1,0:T(8,128)(2,1)S(1)} fusion(bf16[3200,2048]{1,0:T(8,128)(2,1)} %all-gather.6.cloned.1.call-done, bf16[512,3200]{0,1:T(8,128)(2,1)S(1)} %constant_dynamic-update-slice_fusion, f32[3200]{0:T(1024)S(1)} %mul.106, f32[512]{0:T(512)S(1)} %add_rsqrt_fusion.2), kind=kOutput, calls=%fused_computation.34 | convolution fusion | flops 3362521088 | bytes 10893824 | tf_op jit(solution)/shard_map/dot_general | solution.py:87
  265.8 0.3 collective-permute-start.3
  266.1 0.0 copy-done.2
  266.1 15.0 %fusion.51 = (f32[8,512]{1,0:T(8,128)S(1)}, f32[8,512,640]{2,1,0:T(8,128)}) fusion(f32[8,512,640]{2,1,0:T(8,128)} %fusion.31, pred[512,640]{1,0:T(8,128)(4,1)S(1)} %copy-done.2), kind=kOutput, calls=%fused_computation.69 | output fusion | flops 15729279 | bytes 21315584 | tf_op jit(solution)/shard_map/sub | solution.py:85
  281.1 0.0 collective-permute-done.3
  281.1 0.1 pad_maximum_fusion
  281.2 1.0 copy.18
  282.2 0.0 copy-start.3
  282.2 6.0 %fusion.27 = bf16[8,128,512]{2,1,0:T(8,128)(2,1)S(1)} fusion(bf16[640,8,128]{0,2,1:T(8,128)(2,1)S(1)} %bitcast.61, f32[8,512,640]{2,1,0:T(8,128)} %get-tuple-element.23, f32[8,512]{1,0:T(8,128)S(1)} %get-tuple-element.22), kind=kOutput, calls=%fused_computation.33 | convolution fusion | flops 676855808 | bytes 12861440 | tf_op jit(solution)/shard_map/hqk,khd->qhd/dot_general | solution.py:91
  288.2 1.3 collective-permute-start.6
  289.4 0.0 copy-done.3
  289.5 1.2 reduce-window.6
  290.6 0.2 slice_reduce_fusion
  290.9 0.1 fusion.42
  291.0 0.0 copy-start.8
  291.0 5.0 %fusion.19 = bf16[512,1600]{0,1:T(8,128)(2,1)} fusion(bf16[512,1024]{0,1:T(8,128)(2,1)S(1)} %bitcast.68, bf16[3200,2048]{1,0:T(8,128)(2,1)} %all-gather.6.cloned.1.call-done), kind=kOutput, calls=%fused_computation.26 | convolution fusion | flops 1678540800 | bytes 5963776 | tf_op jit(solution)/shard_map/dot_general | solution.py:96
  296.0 16.8 %collective-permute-done.6 = bf16[512,1024]{0,1:T(8,128)(2,1)S(1)} collective-permute-done((bf16[512,1024]{0,1:T(8,128)(2,1)S(1)}, bf16[512,1024]{0,1:T(8,128)(2,1)S(1)}, u32[]{:S(2)}, u32[]{:S(2)}) %collective-permute-start.6) | collective-permute-done | bytes 1048608 | tf_op jit(solution)/shard_map/ppermute | solution.py:19
  312.8 8.5 %convolution_convert_fusion = bf16[1024,1600]{0,1:T(8,128)(2,1)} fusion(s32[512]{0:T(512)S(1)} %multiply_add_fusion, bf16[512,1600]{0,1:T(8,128)(2,1)} %fusion.19, bf16[512,1600]{0,1:T(8,128)(2,1)} %param.8, bf16[512,1024]{0,1:T(8,128)(2,1)S(1)} %collective-permute-done.6, bf16[3200,2048]{1,0:T(8,128)(2,1)} %all-gather.6.cloned.1.call-done, ...), kind=kOutput, calls=%fused_computation.20 | convolution fusion | flops 3364159488 | bytes 10887424 | tf_op jit(solution)/shard_map/dot_general | solution.py:112
  321.3 4.3 %copy.17 = bf16[1024,1600]{1,0:T(8,128)(2,1)S(1)} copy(bf16[1024,1600]{0,1:T(8,128)(2,1)} %convolution_convert_fusion) | data formatting | bytes 6553600 | tf_op jit(solution)/shard_map/convert_element_type | solution.py:112
  325.6 80.4 %all_to_all.5 = bf16[16,64,1600]{2,1,0:T(8,128)(2,1)S(1)} all-to-all(bf16[16,64,1600]{2,1,0:T(8,128)(2,1)S(1)} %bitcast.59), channel_id=1, replica_groups=mesh['group'=16,'tp'=2] {'group'}, dimensions={0} | all-to-all | bytes 6553600 | tf_op jit(solution)/shard_map/all_to_all | solution.py:114
  406.1 1.8 copy.36
  (20 shorter events, 0.2 us)
Async XLA Ops:
  6.5 87.3 %all-gather.8.cloned.1.call-start = ((), (), s32[]{:S(2)}) async-start(), calls=%async_computation.2 | async-start | bytes 6963200 | tf_op jit(solution)/shard_map/all_gather | solution.py:29
  8.9 145.3 %all-gather.10.cloned.1.call-start = ((), (), s32[]{:S(2)}) async-start(), calls=%async_computation.3 | async-start | bytes 6963200 | tf_op jit(solution)/shard_map/all_gather | solution.py:29
  9.6 249.4 %all-gather.6.cloned.1.call-start = ((), (), s32[]{:S(2)}) async-start(), calls=%async_computation.1 | async-start | bytes 13926400 | tf_op jit(solution)/shard_map/all_gather | solution.py:51
  9.7 38.0 %collective-permute-start = (bf16[512,1600]{0,1:T(8,128)(2,1)}, bf16[512,1600]{0,1:T(8,128)(2,1)}, u32[]{:S(2)}, u32[]{:S(2)}) collective-permute-start(bf16[512,1600]{0,1:T(8,128)(2,1)} %param.8), channel_id=1, source_target_pairs={{1,0},{0,1},{3,2},{2,3},{5,4},{4,5},{7,6},{6,7},{9,8},{8,9},{11,10... | collective-permute-start | bytes 4915208 | tf_op jit(solution)/shard_map/ppermute | solution.py:19
  12.0 37.2 %copy-start.7 = (bf16[1024,200]{0,1:T(8,128)(2,1)S(1)}, bf16[1024,200]{0,1:T(8,128)(2,1)}, u32[]{:S(2)}) copy-start(bf16[1024,200]{0,1:T(8,128)(2,1)} %param.12) | copy-start | bytes 1228804
  12.0 37.9 %copy-start.1 = (bf16[200,1024]{1,0:T(8,128)(2,1)S(1)}, bf16[200,1024]{1,0:T(8,128)(2,1)}, u32[]{:S(2)}) copy-start(bf16[200,1024]{1,0:T(8,128)(2,1)} %get-tuple-element.9) | copy-start | bytes 1228804
  13.7 37.2 %copy-start.4 = (bf16[1600]{0:T(1024)(128)(2,1)S(1)}, bf16[1600]{0:T(1024)(128)(2,1)}, u32[]{:S(2)}) copy-start(bf16[1600]{0:T(1024)(128)(2,1)} %param.9) | copy-start | bytes 9604
  13.7 77.2 %copy-start.5 = (s32[512]{0:T(512)S(1)}, s32[512]{0:T(512)}, u32[]{:S(2)}) copy-start(s32[512]{0:T(512)} %param.14) | copy-start | bytes 6148
  13.7 78.2 %copy-start.6 = (f32[2,1024]{1,0:T(2,128)S(1)}, f32[2,1024]{1,0:T(2,128)}, u32[]{:S(2)}) copy-start(f32[2,1024]{1,0:T(2,128)} %param.11) | copy-start | bytes 24580
  49.2 0.7 collective-permute-start.2
  50.9 41.8 %collective-permute-start.1 = (bf16[1,1600]{1,0:T(2,128)(2,1)S(1)}, bf16[1,1600]{1,0:T(2,128)(2,1)S(1)}, u32[]{:S(2)}, u32[]{:S(2)}) collective-permute-start(bf16[1,1600]{1,0:T(2,128)(2,1)S(1)} %reshape.93), channel_id=1, source_target_pairs={{1,0},{0,1},{3,2},{2,3},{5,4},{4,5},{7,6},{6,7},{9,8},{8,9},{11,10... | collective-permute-start | bytes 9608 | tf_op jit(solution)/shard_map/ppermute | solution.py:19
  91.0 1.7 collective-permute-start.4
  166.5 4.3 %copy-start = (f32[512,1024]{1,0:T(8,128)S(1)}, f32[512,1024]{1,0:T(8,128)}, u32[]{:S(2)}) copy-start(f32[512,1024]{1,0:T(8,128)} %get-tuple-element.21) | copy-start | bytes 6291460
  168.5 2.2 collective-permute-start.5
  259.0 7.1 %copy-start.2 = (pred[512,640]{1,0:T(8,128)(4,1)S(1)}, pred[512,640]{1,0:T(8,128)(4,1)}, u32[]{:S(2)}) copy-start(pred[512,640]{1,0:T(8,128)(4,1)} %broadcast_compare_fusion) | copy-start | bytes 983044
  265.8 15.4 %collective-permute-start.3 = (bf16[128,1024]{1,0:T(8,128)(2,1)S(1)}, bf16[128,1024]{1,0:T(8,128)(2,1)S(1)}, u32[]{:S(2)}, u32[]{:S(2)}) collective-permute-start(bf16[128,1024]{1,0:T(8,128)(2,1)S(1)} %constant_dynamic-slice_fusion.1), channel_id=1, source_target_pairs={{0,2},{2,0},{4,6},{6,4},{8,10},{10,8},{12,14},{14,12},{16,18},{18,... | collective-permute-start | bytes 786440 | tf_op jit(solution)/shard_map/ppermute | solution.py:14
  282.2 7.2 %copy-start.3 = (s32[512,1]{0,1:T(1,128)S(1)}, s32[512,1]{0,1:T(1,128)}, u32[]{:S(2)}) copy-start(s32[512,1]{0,1:T(1,128)} %param.15) | copy-start | bytes 6148
  288.2 24.6 %collective-permute-start.6 = (bf16[512,1024]{0,1:T(8,128)(2,1)S(1)}, bf16[512,1024]{0,1:T(8,128)(2,1)S(1)}, u32[]{:S(2)}, u32[]{:S(2)}) collective-permute-start(bf16[512,1024]{0,1:T(8,128)(2,1)S(1)} %bitcast.67), channel_id=1, source_target_pairs={{1,0},{0,1},{3,2},{2,3},{5,4},{4,5},{7,6},{6,7},{9,8},{8,9},{11,10... | collective-permute-start | bytes 3145736 | tf_op jit(solution)/shard_map/ppermute | solution.py:19
  291.0 21.8 %copy-start.8 = (f32[1600]{0:T(1024)S(1)}, f32[1600]{0:T(1024)}, u32[]{:S(2)}) copy-start(f32[1600]{0:T(1024)} %param.13) | copy-start | bytes 19204
Sparse Core Ops, SparseCore 0:
  9.6 65.8 all-gather.7
  77.9 76.2 all-gather.9
  156.4 102.5 all-gather.5
